TPU v7x, 256 devices: a whole 4x4x8 slice. The times are simulated.
256 devices in a mesh: ctx: 128 (over x, z, y_lo, core), head: 2 (over y_hi).
Axes of the slice: x: 4, y: 4 (y_hi: 2, y_lo: 2; y = y_hi * 2 + y_lo), z: 8, core: 2. Of those that a mesh axis runs over, the one named last changes fastest.
Arguments:
- queries: bfloat16 [32768, 512], P('ctx', 'head'), parts along dimension 1, may hold values from -32 to 32
- keys: bfloat16 [32768, 256], P('ctx', 'head'), parts along dimension 1, may hold values from -16 to 16
- values: bfloat16 [32768, 256], P('ctx', 'head'), parts along dimension 1, may hold values from -6 to 6
- doc_starts: int32 [6], P('head'), parts along dimension 0, may hold values from 1 to 12288, as said below
Outputs:
- attended: bfloat16 [32768, 512], P('ctx', 'head'), parts along dimension 1
There are 2 independent parts, one for each index of `head`. A program takes and returns all parts, laid end to end along the dimension named above; each array names one. Nothing has to cross between parts.
Inputs may be any that keep to these rules, and one draw needn't show every extreme that they name: `doc_starts`: strictly rising; the fourth document starts at exactly 12288.
All inputs are finite; a program needn't handle non-finite values.
Results may differ from a plain program's by a relative error of at most 0.01.
Values may be sent and summed in bfloat16 or wider, within the bound.
A program may use at most 64 MiB of HBM per device.

v0:
```python
import math

import jax
import jax.numpy as jnp
from jax import lax
from jax.sharding import PartitionSpec as P

D_HEAD = 128
Q_HEADS = 2


SCALE = 144.0 ** (-0.5)
NEGATIVE = -1e30


def doc_index(positions, doc_starts):
    return jnp.sum((positions[:, None] >= doc_starts[None, :]).astype(jnp.int32), axis=1)


def update_part(partial_value, target, key_block, block_start, doc_starts):
    query_rows, query_pos, query_doc, low_edge, high_edge = target
    key_count = key_block.shape[1]

    def attend(carried):
        row_max, row_total, weighted = carried
        key_pos = block_start + lax.iota(jnp.int32, key_count)
        key_doc = doc_index(key_pos, doc_starts)
        scores = (
            jnp.einsum("qhd,kd->hqk", query_rows, key_block[0], preferred_element_type=jnp.float32)
            * SCALE
        )
        visible = (key_pos[None, :] <= query_pos[:, None]) & (key_pos[None, :] >= low_edge)
        visible = (
            visible & (key_pos[None, :] < high_edge) & (key_doc[None, :] == query_doc[:, None])
        )
        scores = jnp.where(visible[None], scores, NEGATIVE)
        new_max = jnp.maximum(row_max, jnp.max(scores, axis=2))
        expo = jnp.where(visible[None], jnp.exp(scores - new_max[:, :, None]), 0.0)
        rescale = jnp.exp(row_max - new_max)
        row_total = row_total * rescale + jnp.sum(expo, axis=2)
        product = jnp.einsum(
            "hqk,kd->qhd",
            expo.astype(jnp.bfloat16),
            key_block[1],
            preferred_element_type=jnp.float32,
        )
        weighted = weighted * jnp.transpose(rescale)[:, :, None] + product
        return (new_max, row_total, weighted)

    needed = (block_start < high_edge) & (block_start + key_count > low_edge)
    return lax.cond(needed, attend, lambda carried: carried, partial_value)


def shards(queries, keys, values, doc_starts):
    shard_rows = queries.shape[0]
    my_index = lax.axis_index("ctx")
    row_iota = lax.iota(jnp.int32, shard_rows)
    own_pos = my_index * shard_rows + row_iota
    own_rows = queries.reshape(shard_rows, Q_HEADS, D_HEAD)
    own_doc = doc_index(own_pos, doc_starts)
    key_values = jnp.stack([keys, values])
    fresh_partial = (
        jnp.full((Q_HEADS, shard_rows), NEGATIVE, jnp.float32),
        jnp.zeros((Q_HEADS, shard_rows), jnp.float32),
        jnp.zeros((shard_rows, Q_HEADS, D_HEAD), jnp.float32),
    )
    targets = ((own_rows, own_pos, own_doc, jnp.int32(0), (my_index + 1) * shard_rows),)
    partials = tuple((fresh_partial for target in targets))
    shard_keys = lax.all_gather(key_values, "ctx", axis=1, tiled=True)
    key_total = shard_keys.shape[1]
    block_len = shard_rows * math.gcd(key_total // shard_rows, 4)

    def block_step(block_number, running):
        key_block = lax.dynamic_slice_in_dim(shard_keys, block_number * block_len, block_len, 1)
        block_start = block_number * block_len
        return tuple(
            (
                update_part(partial_value, target, key_block, block_start, doc_starts)
                for partial_value, target in zip(running, targets)
            )
        )

    partials = lax.fori_loop(0, key_total // block_len, block_step, partials)
    result = partials[0]
    row_max, row_total, weighted = result
    attended = weighted / jnp.transpose(row_total)[:, :, None]
    return attended.reshape(shard_rows, Q_HEADS * D_HEAD).astype(jnp.bfloat16)


def solution(mesh):
    in_specs = (P("ctx", "head"), P("ctx", "head"), P("ctx", "head"), P("head"))
    out_specs = P("ctx", "head")
    return jax.shard_map(shards, mesh=mesh, in_specs=in_specs, out_specs=out_specs, check_vma=False)
```

profile of v0, /device:TPU:230, one launch (start us, length us, event | category | flops | bytes accessed | tf_op | source)
XLA Modules:
  0.0 432.7 jit_solution(961604463259147152)
XLA Ops:
  10.0 225.3 %all-gather.2.cloned.1.call-done = bf16[2,32768,128]{2,1,0:T(8,128)(2,1)} async-done(((bf16[2,256,128]{2,1,0:T(8,128)(2,1)}), bf16[2,32768,128]{2,1,0:T(8,128)(2,1)}) %all-gather.2.cloned.1.call-update) | async-done | bytes 16777232 | tf_op jit(solution)/shard_map/all_gather | solution.py:69
  235.3 189.7 %while.18 = (s32[]{:T(128)}, f32[2,256]{1,0:T(2,128)S(1)}, f32[2,256]{1,0:T(2,128)S(1)}, f32[256,2,128]{2,0,1:T(8,128)S(1)}, s32[]{:T(128)}, /*index=5*/s32[3]{0...) while((s32[]{:T(128)}, f32[2,256]{1,0:T(2,128)S(1)}, ...), condition=%wide.region_7.8_spmd.clone, body=%wide.region_1.7_spmd.clone.sunk | while | flops 276707072 | bytes 8582549 | solution.py:83
  241.3 5.9 %conditional.3 = ((f32[2,256]{1,0:T(2,128)S(1)}, f32[2,256]{1,0:T(2,128)S(1)}, f32[256,2,128]{2,0,1:T(8,128)S(1)})) conditional(s32[]{:T(128)} %convert_element_type.37, (f32[2,256]{1,0:T(2,128)S(1)}, f32[2,256]{1,0:T(2,128)S(1)}, f32[256,2,128]{2,0,1:T(8,128)S(1)}) %tuple.50, (s32[]{:T(128)}, s32[]{:T(128)}, s32[]{:T(128)}, s32[3]{0:T(128)}, ...), branch_computations={%region_2.0_spmd, %region_3.6_spmd} | conditional | flops 276707072 | bytes 8581238 | solution.py:51
  247.2 5.9 %conditional.3 = ((f32[2,256]{1,0:T(2,128)S(1)}, f32[2,256]{1,0:T(2,128)S(1)}, f32[256,2,128]{2,0,1:T(8,128)S(1)})) conditional(s32[]{:T(128)} %convert_element_type.37, (f32[2,256]{1,0:T(2,128)S(1)}, f32[2,256]{1,0:T(2,128)S(1)}, f32[256,2,128]{2,0,1:T(8,128)S(1)}) %tuple.50, (s32[]{:T(128)}, s32[]{:T(128)}, s32[]{:T(128)}, s32[3]{0:T(128)}, ...), branch_computations={%region_2.0_spmd, %region_3.6_spmd} | conditional | flops 276707072 | bytes 8581238 | solution.py:51
  253.1 5.9 %conditional.3 = ((f32[2,256]{1,0:T(2,128)S(1)}, f32[2,256]{1,0:T(2,128)S(1)}, f32[256,2,128]{2,0,1:T(8,128)S(1)})) conditional(s32[]{:T(128)} %convert_element_type.37, (f32[2,256]{1,0:T(2,128)S(1)}, f32[2,256]{1,0:T(2,128)S(1)}, f32[256,2,128]{2,0,1:T(8,128)S(1)}) %tuple.50, (s32[]{:T(128)}, s32[]{:T(128)}, s32[]{:T(128)}, s32[3]{0:T(128)}, ...), branch_computations={%region_2.0_spmd, %region_3.6_spmd} | conditional | flops 276707072 | bytes 8581238 | solution.py:51
  259.1 5.9 %conditional.3 = ((f32[2,256]{1,0:T(2,128)S(1)}, f32[2,256]{1,0:T(2,128)S(1)}, f32[256,2,128]{2,0,1:T(8,128)S(1)})) conditional(s32[]{:T(128)} %convert_element_type.37, (f32[2,256]{1,0:T(2,128)S(1)}, f32[2,256]{1,0:T(2,128)S(1)}, f32[256,2,128]{2,0,1:T(8,128)S(1)}) %tuple.50, (s32[]{:T(128)}, s32[]{:T(128)}, s32[]{:T(128)}, s32[3]{0:T(128)}, ...), branch_computations={%region_2.0_spmd, %region_3.6_spmd} | conditional | flops 276707072 | bytes 8581238 | solution.py:51
  265.0 5.9 %conditional.3 = ((f32[2,256]{1,0:T(2,128)S(1)}, f32[2,256]{1,0:T(2,128)S(1)}, f32[256,2,128]{2,0,1:T(8,128)S(1)})) conditional(s32[]{:T(128)} %convert_element_type.37, (f32[2,256]{1,0:T(2,128)S(1)}, f32[2,256]{1,0:T(2,128)S(1)}, f32[256,2,128]{2,0,1:T(8,128)S(1)}) %tuple.50, (s32[]{:T(128)}, s32[]{:T(128)}, s32[]{:T(128)}, s32[3]{0:T(128)}, ...), branch_computations={%region_2.0_spmd, %region_3.6_spmd} | conditional | flops 276707072 | bytes 8581238 | solution.py:51
  270.9 5.9 %conditional.3 = ((f32[2,256]{1,0:T(2,128)S(1)}, f32[2,256]{1,0:T(2,128)S(1)}, f32[256,2,128]{2,0,1:T(8,128)S(1)})) conditional(s32[]{:T(128)} %convert_element_type.37, (f32[2,256]{1,0:T(2,128)S(1)}, f32[2,256]{1,0:T(2,128)S(1)}, f32[256,2,128]{2,0,1:T(8,128)S(1)}) %tuple.50, (s32[]{:T(128)}, s32[]{:T(128)}, s32[]{:T(128)}, s32[3]{0:T(128)}, ...), branch_computations={%region_2.0_spmd, %region_3.6_spmd} | conditional | flops 276707072 | bytes 8581238 | solution.py:51
  276.8 5.9 %conditional.3 = ((f32[2,256]{1,0:T(2,128)S(1)}, f32[2,256]{1,0:T(2,128)S(1)}, f32[256,2,128]{2,0,1:T(8,128)S(1)})) conditional(s32[]{:T(128)} %convert_element_type.37, (f32[2,256]{1,0:T(2,128)S(1)}, f32[2,256]{1,0:T(2,128)S(1)}, f32[256,2,128]{2,0,1:T(8,128)S(1)}) %tuple.50, (s32[]{:T(128)}, s32[]{:T(128)}, s32[]{:T(128)}, s32[3]{0:T(128)}, ...), branch_computations={%region_2.0_spmd, %region_3.6_spmd} | conditional | flops 276707072 | bytes 8581238 | solution.py:51
  282.8 5.9 %conditional.3 = ((f32[2,256]{1,0:T(2,128)S(1)}, f32[2,256]{1,0:T(2,128)S(1)}, f32[256,2,128]{2,0,1:T(8,128)S(1)})) conditional(s32[]{:T(128)} %convert_element_type.37, (f32[2,256]{1,0:T(2,128)S(1)}, f32[2,256]{1,0:T(2,128)S(1)}, f32[256,2,128]{2,0,1:T(8,128)S(1)}) %tuple.50, (s32[]{:T(128)}, s32[]{:T(128)}, s32[]{:T(128)}, s32[3]{0:T(128)}, ...), branch_computations={%region_2.0_spmd, %region_3.6_spmd} | conditional | flops 276707072 | bytes 8581238 | solution.py:51
  288.7 5.9 %conditional.3 = ((f32[2,256]{1,0:T(2,128)S(1)}, f32[2,256]{1,0:T(2,128)S(1)}, f32[256,2,128]{2,0,1:T(8,128)S(1)})) conditional(s32[]{:T(128)} %convert_element_type.37, (f32[2,256]{1,0:T(2,128)S(1)}, f32[2,256]{1,0:T(2,128)S(1)}, f32[256,2,128]{2,0,1:T(8,128)S(1)}) %tuple.50, (s32[]{:T(128)}, s32[]{:T(128)}, s32[]{:T(128)}, s32[3]{0:T(128)}, ...), branch_computations={%region_2.0_spmd, %region_3.6_spmd} | conditional | flops 276707072 | bytes 8581238 | solution.py:51
  294.6 5.9 %conditional.3 = ((f32[2,256]{1,0:T(2,128)S(1)}, f32[2,256]{1,0:T(2,128)S(1)}, f32[256,2,128]{2,0,1:T(8,128)S(1)})) conditional(s32[]{:T(128)} %convert_element_type.37, (f32[2,256]{1,0:T(2,128)S(1)}, f32[2,256]{1,0:T(2,128)S(1)}, f32[256,2,128]{2,0,1:T(8,128)S(1)}) %tuple.50, (s32[]{:T(128)}, s32[]{:T(128)}, s32[]{:T(128)}, s32[3]{0:T(128)}, ...), branch_computations={%region_2.0_spmd, %region_3.6_spmd} | conditional | flops 276707072 | bytes 8581238 | solution.py:51
  300.6 5.9 %conditional.3 = ((f32[2,256]{1,0:T(2,128)S(1)}, f32[2,256]{1,0:T(2,128)S(1)}, f32[256,2,128]{2,0,1:T(8,128)S(1)})) conditional(s32[]{:T(128)} %convert_element_type.37, (f32[2,256]{1,0:T(2,128)S(1)}, f32[2,256]{1,0:T(2,128)S(1)}, f32[256,2,128]{2,0,1:T(8,128)S(1)}) %tuple.50, (s32[]{:T(128)}, s32[]{:T(128)}, s32[]{:T(128)}, s32[3]{0:T(128)}, ...), branch_computations={%region_2.0_spmd, %region_3.6_spmd} | conditional | flops 276707072 | bytes 8581238 | solution.py:51
  306.5 5.9 %conditional.3 = ((f32[2,256]{1,0:T(2,128)S(1)}, f32[2,256]{1,0:T(2,128)S(1)}, f32[256,2,128]{2,0,1:T(8,128)S(1)})) conditional(s32[]{:T(128)} %convert_element_type.37, (f32[2,256]{1,0:T(2,128)S(1)}, f32[2,256]{1,0:T(2,128)S(1)}, f32[256,2,128]{2,0,1:T(8,128)S(1)}) %tuple.50, (s32[]{:T(128)}, s32[]{:T(128)}, s32[]{:T(128)}, s32[3]{0:T(128)}, ...), branch_computations={%region_2.0_spmd, %region_3.6_spmd} | conditional | flops 276707072 | bytes 8581238 | solution.py:51
  312.4 5.9 %conditional.3 = ((f32[2,256]{1,0:T(2,128)S(1)}, f32[2,256]{1,0:T(2,128)S(1)}, f32[256,2,128]{2,0,1:T(8,128)S(1)})) conditional(s32[]{:T(128)} %convert_element_type.37, (f32[2,256]{1,0:T(2,128)S(1)}, f32[2,256]{1,0:T(2,128)S(1)}, f32[256,2,128]{2,0,1:T(8,128)S(1)}) %tuple.50, (s32[]{:T(128)}, s32[]{:T(128)}, s32[]{:T(128)}, s32[3]{0:T(128)}, ...), branch_computations={%region_2.0_spmd, %region_3.6_spmd} | conditional | flops 276707072 | bytes 8581238 | solution.py:51
  318.3 5.9 %conditional.3 = ((f32[2,256]{1,0:T(2,128)S(1)}, f32[2,256]{1,0:T(2,128)S(1)}, f32[256,2,128]{2,0,1:T(8,128)S(1)})) conditional(s32[]{:T(128)} %convert_element_type.37, (f32[2,256]{1,0:T(2,128)S(1)}, f32[2,256]{1,0:T(2,128)S(1)}, f32[256,2,128]{2,0,1:T(8,128)S(1)}) %tuple.50, (s32[]{:T(128)}, s32[]{:T(128)}, s32[]{:T(128)}, s32[3]{0:T(128)}, ...), branch_computations={%region_2.0_spmd, %region_3.6_spmd} | conditional | flops 276707072 | bytes 8581238 | solution.py:51
  324.3 5.9 %conditional.3 = ((f32[2,256]{1,0:T(2,128)S(1)}, f32[2,256]{1,0:T(2,128)S(1)}, f32[256,2,128]{2,0,1:T(8,128)S(1)})) conditional(s32[]{:T(128)} %convert_element_type.37, (f32[2,256]{1,0:T(2,128)S(1)}, f32[2,256]{1,0:T(2,128)S(1)}, f32[256,2,128]{2,0,1:T(8,128)S(1)}) %tuple.50, (s32[]{:T(128)}, s32[]{:T(128)}, s32[]{:T(128)}, s32[3]{0:T(128)}, ...), branch_computations={%region_2.0_spmd, %region_3.6_spmd} | conditional | flops 276707072 | bytes 8581238 | solution.py:51
  330.2 5.9 %conditional.3 = ((f32[2,256]{1,0:T(2,128)S(1)}, f32[2,256]{1,0:T(2,128)S(1)}, f32[256,2,128]{2,0,1:T(8,128)S(1)})) conditional(s32[]{:T(128)} %convert_element_type.37, (f32[2,256]{1,0:T(2,128)S(1)}, f32[2,256]{1,0:T(2,128)S(1)}, f32[256,2,128]{2,0,1:T(8,128)S(1)}) %tuple.50, (s32[]{:T(128)}, s32[]{:T(128)}, s32[]{:T(128)}, s32[3]{0:T(128)}, ...), branch_computations={%region_2.0_spmd, %region_3.6_spmd} | conditional | flops 276707072 | bytes 8581238 | solution.py:51
  336.1 5.9 %conditional.3 = ((f32[2,256]{1,0:T(2,128)S(1)}, f32[2,256]{1,0:T(2,128)S(1)}, f32[256,2,128]{2,0,1:T(8,128)S(1)})) conditional(s32[]{:T(128)} %convert_element_type.37, (f32[2,256]{1,0:T(2,128)S(1)}, f32[2,256]{1,0:T(2,128)S(1)}, f32[256,2,128]{2,0,1:T(8,128)S(1)}) %tuple.50, (s32[]{:T(128)}, s32[]{:T(128)}, s32[]{:T(128)}, s32[3]{0:T(128)}, ...), branch_computations={%region_2.0_spmd, %region_3.6_spmd} | conditional | flops 276707072 | bytes 8581238 | solution.py:51
  342.1 5.9 %conditional.3 = ((f32[2,256]{1,0:T(2,128)S(1)}, f32[2,256]{1,0:T(2,128)S(1)}, f32[256,2,128]{2,0,1:T(8,128)S(1)})) conditional(s32[]{:T(128)} %convert_element_type.37, (f32[2,256]{1,0:T(2,128)S(1)}, f32[2,256]{1,0:T(2,128)S(1)}, f32[256,2,128]{2,0,1:T(8,128)S(1)}) %tuple.50, (s32[]{:T(128)}, s32[]{:T(128)}, s32[]{:T(128)}, s32[3]{0:T(128)}, ...), branch_computations={%region_2.0_spmd, %region_3.6_spmd} | conditional | flops 276707072 | bytes 8581238 | solution.py:51
  348.0 5.9 %conditional.3 = ((f32[2,256]{1,0:T(2,128)S(1)}, f32[2,256]{1,0:T(2,128)S(1)}, f32[256,2,128]{2,0,1:T(8,128)S(1)})) conditional(s32[]{:T(128)} %convert_element_type.37, (f32[2,256]{1,0:T(2,128)S(1)}, f32[2,256]{1,0:T(2,128)S(1)}, f32[256,2,128]{2,0,1:T(8,128)S(1)}) %tuple.50, (s32[]{:T(128)}, s32[]{:T(128)}, s32[]{:T(128)}, s32[3]{0:T(128)}, ...), branch_computations={%region_2.0_spmd, %region_3.6_spmd} | conditional | flops 276707072 | bytes 8581238 | solution.py:51
  353.9 5.9 %conditional.3 = ((f32[2,256]{1,0:T(2,128)S(1)}, f32[2,256]{1,0:T(2,128)S(1)}, f32[256,2,128]{2,0,1:T(8,128)S(1)})) conditional(s32[]{:T(128)} %convert_element_type.37, (f32[2,256]{1,0:T(2,128)S(1)}, f32[2,256]{1,0:T(2,128)S(1)}, f32[256,2,128]{2,0,1:T(8,128)S(1)}) %tuple.50, (s32[]{:T(128)}, s32[]{:T(128)}, s32[]{:T(128)}, s32[3]{0:T(128)}, ...), branch_computations={%region_2.0_spmd, %region_3.6_spmd} | conditional | flops 276707072 | bytes 8581238 | solution.py:51
  359.8 5.9 %conditional.3 = ((f32[2,256]{1,0:T(2,128)S(1)}, f32[2,256]{1,0:T(2,128)S(1)}, f32[256,2,128]{2,0,1:T(8,128)S(1)})) conditional(s32[]{:T(128)} %convert_element_type.37, (f32[2,256]{1,0:T(2,128)S(1)}, f32[2,256]{1,0:T(2,128)S(1)}, f32[256,2,128]{2,0,1:T(8,128)S(1)}) %tuple.50, (s32[]{:T(128)}, s32[]{:T(128)}, s32[]{:T(128)}, s32[3]{0:T(128)}, ...), branch_computations={%region_2.0_spmd, %region_3.6_spmd} | conditional | flops 276707072 | bytes 8581238 | solution.py:51
  365.8 5.9 %conditional.3 = ((f32[2,256]{1,0:T(2,128)S(1)}, f32[2,256]{1,0:T(2,128)S(1)}, f32[256,2,128]{2,0,1:T(8,128)S(1)})) conditional(s32[]{:T(128)} %convert_element_type.37, (f32[2,256]{1,0:T(2,128)S(1)}, f32[2,256]{1,0:T(2,128)S(1)}, f32[256,2,128]{2,0,1:T(8,128)S(1)}) %tuple.50, (s32[]{:T(128)}, s32[]{:T(128)}, s32[]{:T(128)}, s32[3]{0:T(128)}, ...), branch_computations={%region_2.0_spmd, %region_3.6_spmd} | conditional | flops 276707072 | bytes 8581238 | solution.py:51
  (405 shorter events, 248.7 us)
Async XLA Ops:
  6.5 228.7 %all-gather.2.cloned.1.call-start = ((), (), s32[]{:S(2)}) async-start(), calls=%async_computation | async-start | bytes 16908288 | tf_op jit(solution)/shard_map/all_gather | solution.py:69
Sparse Core Ops, SparseCore 0:
  9.2 226.0 all-gather.1
where the time goes:
time: 435 us; the launch traced here: 433 us
  waiting for transfers between devices  225 us (52%)
  matrix products  104 us (24%)
  other arithmetic  84.4 us (19%)
  between operations  13.4 us (3%)
    all_gather x1, waiting for transfers between devices, shards(): shard_keys = lax.all_gather(key_values, 'ctx', axis=1, tiled=True)  225 us
    dot_general x32, matrix products, attend(): jnp.einsum('hqk,kd->qhd', expo.astype(jnp.bfloat16), key_block[1], prefer...  59 us
    dot_general x32, matrix products, attend(): jnp.einsum('qhd,kd->hqk', query_rows, key_block[0], preferred_element_typ...  45.2 us
    and x32, other arithmetic, attend(): visible & (key_pos[None, :] < high_edge)  38.2 us
    reduce_sum x33, other arithmetic, doc_index(): jnp.sum((positions[:, None] >= doc_starts[None, :]).astype(jnp.int32), ax...  24.4 us
    reduce_sum x32, other arithmetic, attend(): row_total = row_total * rescale + jnp.sum(expo, axis=2)  18.1 us
  transfers between devices with their start and end apart: 1, of which 1 were waited for; matrix products, arithmetic and copies ran while one was open for 0% of the time, Pallas kernels for 0%

commit v1 on v0

v1 whole, which is shorter than its diff:
```python
import functools
import math

import jax
import jax.numpy as jnp
from jax import lax
from jax.experimental import pallas as pl
from jax.experimental.pallas import tpu as pltpu
from jax.sharding import PartitionSpec as P

D = 128
H = 2
NX, NZ, NY, NC = 4, 8, 2, 2
PLANE = NZ * NY * NC
EDGE = 48
NEG = -1e30
C2 = math.log2(math.e) / 12.0
SENDS = 31


def ctx_of(x, z, y, c):
    return ((x * NZ + z) * NY + y) * NC + c


def kernel(
    docs, q_in, k_in, v_in, out,
    qbuf, kbuf, vbuf, acc, mx, tot, osend, ssend, orecv, srecv,
    ksem, vsem, qsem, osem, rsem, ksent, vsent, qsent, osent, rsent,
):
    sh = k_in.shape[0]
    grp = NY * NC * sh
    me = lax.axis_index("ctx")
    x = me // PLANE
    z = (me // (NY * NC)) % NZ
    y = (me // NC) % NY
    c = me % NC
    up = ctx_of(x, (z + 1) % NZ, y, c)
    down = ctx_of(x, (z + NZ - 1) % NZ, y, c)
    across = ctx_of(x, z, 1 - y, c)
    twin = ctx_of(x, z, y, 1 - c)

    def shard(zz, yy, cc):
        return (zz * NY + yy) * NC + cc

    def rows(j):
        return pl.ds(pl.multiple_of(j * sh, sh), sh)

    def send(src, dst, sent, got, to):
        return pltpu.make_async_remote_copy(
            src_ref=src, dst_ref=dst, send_sem=sent, recv_sem=got,
            device_id={"ctx": to}, device_id_type=pl.DeviceIdType.MESH,
        )

    def k_send(j, to, src=None):
        send(kbuf.at[rows(j)] if src is None else src, kbuf.at[rows(j)], ksent, ksem.at[j], to).start()

    def v_send(j, to, src=None):
        send(vbuf.at[rows(j)] if src is None else src, vbuf.at[rows(j)], vsent, vsem.at[j], to).start()

    def k_wait(j):
        send(kbuf.at[rows(j)], kbuf.at[rows(j)], ksent, ksem.at[j], twin).wait_recv()

    def v_wait(j):
        send(vbuf.at[rows(j)], vbuf.at[rows(j)], vsent, vsem.at[j], twin).wait_recv()

    mine = shard(z, y, c)
    own = [
        pltpu.make_async_copy(q_in, qbuf.at[0], qsem.at[0]),
        pltpu.make_async_copy(k_in, kbuf.at[rows(mine)], ksem.at[mine]),
        pltpu.make_async_copy(v_in, vbuf.at[rows(mine)], vsem.at[mine]),
    ]
    for copy in own:
        copy.start()

    low = z < NZ // 2
    host = {1: (x == 2) | (x == 1) | ((x == 0) & low), 2: x == 1}
    guest = {1: (x == 3) | (x == 2) | ((x == 1) & low), 2: x == 3}

    barrier = pltpu.get_barrier_semaphore()
    partners = [up, down, across, twin]
    partners += [ctx_of((x + step) % NX, z, y, c) for step in (1, 2, 3)]
    for partner in partners:
        pl.semaphore_signal(barrier, inc=1, device_id={"ctx": partner}, device_id_type=pl.DeviceIdType.MESH)

    for slot in range(3):
        for h in range(H):
            mx[slot, h] = jnp.full((sh, D), NEG, jnp.float32)
            tot[slot, h] = jnp.zeros((sh, D), jnp.float32)
            acc[slot, h] = jnp.zeros((sh, D), jnp.float32)

    pl.semaphore_wait(barrier, len(partners))

    k_send(mine, up, k_in)
    k_send(mine, down, k_in)
    k_send(mine, across, k_in)
    v_send(mine, across, v_in)
    for slot in (1, 2):
        @pl.when(guest[slot])
        def _(slot=slot):
            send(q_in, qbuf.at[slot], qsent.at[slot], qsem.at[slot], ctx_of((x + NX - slot) % NX, z, y, c)).start()
    v_send(mine, up, v_in)
    v_send(mine, down, v_in)
    k_send(mine, twin, k_in)
    v_send(mine, twin, v_in)

    cross = shard(z, 1 - y, c)
    v_wait(cross)
    v_send(cross, up)
    v_send(cross, down)
    v_send(cross, twin)
    k_wait(cross)
    k_send(cross, twin)
    for copy in own:
        copy.wait()
    for slot in (1, 2):
        @pl.when(host[slot])
        def _(slot=slot):
            send(q_in, qbuf.at[slot], qsent.at[slot], qsem.at[slot], twin).wait_recv()

    def attend(slot, g, masked):
        k = kbuf[pl.ds(pl.multiple_of(g * grp, grp), grp), :]
        v = vbuf[pl.ds(pl.multiple_of(g * grp, grp), grp), :]
        vv = jnp.concatenate([v, jnp.ones_like(v)], axis=1)
        if masked:
            q0 = ctx_of(x + slot, z, y, c) * sh
            k0 = (x * PLANE + g * NY * NC) * sh
            qpos = q0 + lax.broadcasted_iota(jnp.int32, (sh, D), 0)
            lo = jnp.zeros((sh, D), jnp.int32)
            for i in range(3):
                lo = jnp.where(qpos >= docs[i], docs[i], lo)
            lane = lax.broadcasted_iota(jnp.int32, (sh, D), 1)
        for h in range(H):
            q = qbuf[slot, :, h * D:(h + 1) * D]
            s = lax.dot_general(q, k, (((1,), (1,)), ((), ())), preferred_element_type=jnp.float32)
            parts = [s[:, j * D:(j + 1) * D] for j in range(grp // D)]
            if masked:
                parts = [
                    jnp.where((lane + (k0 + j * D) <= qpos) & (lane + (k0 + j * D) >= lo), part, NEG)
                    for j, part in enumerate(parts)
                ]
            top = functools.reduce(jnp.maximum, parts)
            old = mx[slot, h]
            new = jnp.maximum(old, jnp.max(top, axis=1, keepdims=True))
            new2 = new * C2
            p = jnp.concatenate([jnp.exp2(part * C2 - new2).astype(jnp.bfloat16) for part in parts], axis=1)
            decay = jnp.exp2(old * C2 - new2)
            pv = jnp.dot(p, vv, preferred_element_type=jnp.float32)
            mx[slot, h] = new
            tot[slot, h] = tot[slot, h] * decay + pv[:, D:]
            acc[slot, h] = acc[slot, h] * decay + pv[:, :D]

    def task(slot, g):
        if_own = (slot == 0) & (g <= z) & jnp.logical_not((x == 1) & (z >= NZ // 2) & (g < NZ // 2))
        if_one = (slot == 1) & ((x == 2) | ((x == 1) & (g >= NZ // 2)) | ((x == 0) & low))
        if_two = (slot == 2) & (x == 1) & (g >= NZ // 2)
        needed = if_own | if_one | if_two
        masked = ((slot == 0) & (g == z)) | (x == 0) | ((slot == 0) & (x == 1) & low)

        @pl.when(needed & masked)
        def _():
            attend(slot, g, True)

        @pl.when(needed & jnp.logical_not(masked))
        def _():
            attend(slot, g, False)

    eye = lax.broadcasted_iota(jnp.int32, (D, D), 0) == lax.broadcasted_iota(jnp.int32, (D, D), 1)

    def finish(slot):
        for h in range(H):
            weight = tot[slot, h]
            osend[slot - 1, :, h * D:(h + 1) * D] = (acc[slot, h] / weight).astype(jnp.bfloat16)
            lse = mx[slot, h] * C2 + jnp.log2(weight)
            for b in range(sh // D):
                block = jnp.where(eye, lse[b * D:(b + 1) * D], 0.0)
                ssend[slot - 1, pl.ds(h * (sh // D) + b, 1), :] = jnp.sum(block, axis=0, keepdims=True)

    def o_copies(slot):
        to = ctx_of((x + slot) % NX, z, y, c)
        i = slot - 1
        return (
            send(osend.at[i], orecv.at[i], osent.at[i], osem.at[i], to),
            send(ssend.at[i], srecv.at[i], rsent.at[i], rsem.at[i], to),
        )

    @pl.loop(1, NZ // 2 + 2)
    def _(s):
        up_z = (z + NZ - s) % NZ
        down_z = (z + s) % NZ

        @pl.when(s <= NZ // 2)
        def _():
            j = shard(up_z, y, c)
            k_wait(j)

            @pl.when(s < NZ // 2)
            def _():
                k_send(j, up)
            k_send(j, across)
            k_send(j, twin)

        @pl.when(s < NZ // 2)
        def _():
            j = shard(down_z, y, c)
            k_wait(j)

            @pl.when(s < NZ // 2 - 1)
            def _():
                k_send(j, down)
            k_send(j, across)
            k_send(j, twin)

        for side in (y, 1 - y):
            @pl.when(s < NZ // 2)
            def _(side=side):
                j = shard(up_z, side, c)
                v_wait(j)

                @pl.when(s < NZ // 2 - 1)
                def _():
                    v_send(j, up)
                v_send(j, twin)

            @pl.when(s <= NZ // 2)
            def _(side=side):
                j = shard(down_z, side, c)
                v_wait(j)

                @pl.when(s < NZ // 2)
                def _():
                    v_send(j, down)
                v_send(j, twin)

        r = s - 1
        first = (z + NZ - r) % NZ
        second = (z + r) % NZ

        @pl.when(r > 0)
        def _():
            j = shard(first, 1 - y, c)
            k_wait(j)
            k_send(j, twin)

        @pl.when((r > 0) & (r < NZ // 2))
        def _():
            j = shard(second, 1 - y, c)
            k_wait(j)
            k_send(j, twin)

        def group(g, final):
            for yy in range(NY):
                k_wait(shard(g, yy, 1 - c))
                v_wait(shard(g, yy, 1 - c))

            @pl.loop(0, 2)
            def _(i):
                task(2 - i, g)

            if final:
                for slot in (1, 2):
                    @pl.when((r == NZ // 2) & host[slot])
                    def _(slot=slot):
                        finish(slot)
                        for copy in o_copies(slot):
                            copy.start()
            task(0, g)

        sides = 2 - ((r == 0) | (r == NZ // 2)).astype(jnp.int32)

        @pl.loop(0, sides)
        def _(i):
            g = first * (1 - i) + second * i
            group(g, True)

    for slot in (1, 2):
        @pl.when(guest[slot])
        def _(slot=slot):
            for copy in o_copies(slot):
                copy.wait_recv()
            send(q_in, qbuf.at[slot], qsent.at[slot], qsem.at[slot], twin).wait_send()

    def merge(slots):
        for h in range(H):
            for b in range(sh // D):
                here = slice(b * D, (b + 1) * D)
                m2 = mx[0, h, here] * C2
                best = m2
                lses = []
                for slot in slots:
                    row = srecv[slot - 1, pl.ds(h * (sh // D) + b, 1), :]
                    col = jnp.sum(jnp.where(eye, row, 0.0), axis=1, keepdims=True)
                    lse = jnp.broadcast_to(col, (D, D))
                    lses.append(lse)
                    best = jnp.maximum(best, lse)
                w = jnp.exp2(m2 - best)
                num = acc[0, h, here] * w
                den = tot[0, h, here] * w
                for slot, lse in zip(slots, lses):
                    w = jnp.exp2(lse - best)
                    num += orecv[slot - 1, here, h * D:(h + 1) * D].astype(jnp.float32) * w
                    den += w
                out[here, h * D:(h + 1) * D] = (num / den).astype(out.dtype)

    @pl.when(guest[2])
    def _():
        merge((1, 2))

    @pl.when(guest[1] & jnp.logical_not(guest[2]))
    def _():
        merge((1,))

    @pl.when(jnp.logical_not(guest[1]))
    def _():
        merge(())

    for slot in (1, 2):
        @pl.when(host[slot])
        def _(slot=slot):
            for copy in o_copies(slot):
                copy.wait_send()
    send(kbuf.at[pl.ds(0, SENDS * sh)], kbuf.at[pl.ds(0, SENDS * sh)], ksent, ksem.at[0], twin).wait_send()
    send(vbuf.at[pl.ds(0, SENDS * sh)], vbuf.at[pl.ds(0, SENDS * sh)], vsent, vsem.at[0], twin).wait_send()


def shards(queries, keys, values, doc_starts):
    sh = keys.shape[0]
    any_spec = pl.BlockSpec(memory_space=pl.ANY)
    dma = pltpu.SemaphoreType.DMA
    return pl.pallas_call(
        kernel,
        out_shape=jax.ShapeDtypeStruct((sh, H * D), jnp.bfloat16),
        in_specs=[pl.BlockSpec(memory_space=pltpu.SMEM), any_spec, any_spec, any_spec],
        out_specs=pl.BlockSpec(memory_space=pltpu.VMEM),
        scratch_shapes=[
            pltpu.VMEM((3, sh, H * D), jnp.bfloat16),
            pltpu.VMEM((PLANE * sh, D), jnp.bfloat16),
            pltpu.VMEM((PLANE * sh, D), jnp.bfloat16),
            pltpu.VMEM((3, H, sh, D), jnp.float32),
            pltpu.VMEM((3, H, sh, D), jnp.float32),
            pltpu.VMEM((3, H, sh, D), jnp.float32),
            pltpu.VMEM((2, sh, H * D), jnp.bfloat16),
            pltpu.VMEM((2, H * sh // D, D), jnp.float32),
            pltpu.VMEM((2, sh, H * D), jnp.bfloat16),
            pltpu.VMEM((2, H * sh // D, D), jnp.float32),
            dma((PLANE,)), dma((PLANE,)), dma((3,)), dma((2,)), dma((2,)),
            dma, dma, dma((3,)), dma((2,)), dma((2,)),
        ],
        compiler_params=pltpu.CompilerParams(collective_id=0, has_side_effects=True),
        name="plane_attention",
    )(doc_starts, queries, keys, values)


def solution(mesh):
    in_specs = (P("ctx", "head"), P("ctx", "head"), P("ctx", "head"), P("head"))
    out_specs = P("ctx", "head")
    return jax.shard_map(shards, mesh=mesh, in_specs=in_specs, out_specs=out_specs, check_vma=False)
```

time: 435 us -> 46.5 us (0.11)
  the two profiles are of different devices: /device:TPU:230 before, /device:TPU:94 now
where the time goes in v1:
time: 46.5 us; the launch traced here: 46.4 us
  Pallas kernels  44.8 us (96%)
  local copies, waits for them, and re-layouts  1.57 us (3%)
    pallas_call x1, Pallas kernels, shards(): pl.pallas_call(kernel, out_shape=jax.ShapeDtypeStruct((sh, H * D), jnp.bf...  44.8 us
    unnamed x1, local copies, waits for them, and re-layouts  1.57 us

profile of v1, /device:TPU:94, one launch (start us, length us, event | category | flops | bytes accessed | tf_op | source)
XLA Modules:
  0.0 46.4 jit_solution(4534462459195249149)
XLA Ops:
  0.0 44.8 %plane_attention.1 = bf16[256,256]{1,0:T(8,128)(2,1)} custom-call(s32[3]{0:T(128)} %docs.1, bf16[256,256]{1,0:T(8,128)(2,1)} %q_in.1, bf16[256,128]{1,0:T(8,128)(2,1)} %k_in.1, bf16[256,128]{1,0:T(8,128)(2,1)} %v_in.1), custom_call_target="tpu_custom_call" | custom-call | tf_op jit(solution)/shard_map/plane_attention/pallas_call | solution.py:329
  44.8 1.6 %copy.6 = bf16[256,256]{1,0:T(8,128)(2,1)} copy(bf16[256,256]{1,0:T(8,128)(2,1)} %plane_attention.1) | data formatting | bytes 262144

commit v2 on v0

v2 whole, which is shorter than its diff:
```python
import functools
import math

import jax
import jax.numpy as jnp
from jax import lax
from jax.experimental import pallas as pl
from jax.experimental.pallas import tpu as pltpu
from jax.sharding import PartitionSpec as P

D = 128
H = 2
NX, NZ, NY, NC = 4, 8, 2, 2
PLANE = NZ * NY * NC
SLOTS = 6
ROWS = 256
BEGIN = (7, 5, 1, 2, 3, 4)
CUT = 2
NEG = -1e30
C2 = math.log2(math.e) / 12.0
SENDS = 26


def ctx_of(x, z, y, c):
    return ((x * NZ + z) * NY + y) * NC + c


def kernel(
    docs, q_in, k_in, v_in, out,
    qbuf, kv, acc, mx, tot, osend, ssend, orecv, srecv,
    kvsem, qsem, osem, rsem, kvsent, first_sent, qsent, osent, rsent,
):
    sh = k_in.shape[0]
    grp = NC * sh
    half = NZ // 2
    piece = sh // CUT
    pieces = 2 * CUT
    vbase = NZ * NC
    me = lax.axis_index("ctx")
    x = me // PLANE
    z = (me // (NY * NC)) % NZ
    y = (me // NC) % NY
    c = me % NC
    up = ctx_of(x, (z + 1) % NZ, y, c)
    down = ctx_of(x, (z + NZ - 1) % NZ, y, c)
    twin = ctx_of(x, z, y, 1 - c)

    def shard(zz, cc):
        return zz * NC + cc

    def rows(j, ch):
        start = (ch // CUT * vbase + j) * sh + ch % CUT * piece
        return pl.ds(pl.multiple_of(start, piece), piece)

    def send(src, dst, sent, got, to):
        return pltpu.make_async_remote_copy(
            src_ref=src, dst_ref=dst, send_sem=sent, recv_sem=got,
            device_id={"ctx": to}, device_id_type=pl.DeviceIdType.MESH,
        )

    def kv_send(j, ch, to):
        send(kv.at[rows(j, ch)], kv.at[rows(j, ch)], kvsent, kvsem.at[j * pieces + ch], to).start()

    def kv_wait(j, ch):
        send(kv.at[rows(j, ch)], kv.at[rows(j, ch)], kvsent, kvsem.at[j * pieces + ch], twin).wait_recv()

    mine = shard(z, c)
    own = [pltpu.make_async_copy(q_in, qbuf.at[0], qsem.at[0])]
    for ch in range(pieces):
        src = (k_in, v_in)[ch // CUT].at[pl.ds(ch % CUT * piece, piece)]
        own.append(pltpu.make_async_copy(src, kv.at[rows(mine, ch)], kvsem.at[mine * pieces + ch]))
    for copy in own:
        copy.start()

    low = z < half
    host = (x >= 0, (x == 2) | (x == 1) | ((x == 0) & low), x == 1)
    guest = (x >= 0, (x == 3) | (x == 2) | ((x == 1) & low), x == 3)

    def hosted(slot):
        sx = slot // 2
        return (sx == 0) | ((sx == 1) & host[1]) | ((sx == 2) & host[2])

    def home(slot):
        side = y + (slot % 2) * (1 - 2 * y)
        return ctx_of((x + slot // 2) % NX, z, side, c)

    def q_copy(slot):
        side = y + (slot % 2) * (1 - 2 * y)
        to = ctx_of((x + NX - slot // 2) % NX, z, side, c)
        return send(q_in, qbuf.at[slot], qsent.at[slot], qsem.at[slot], to)

    barrier = pltpu.get_barrier_semaphore()
    partners = [up, down, twin]
    partners += [ctx_of((x + dx) % NX, z, side, c) for dx in range(NX) for side in (y, 1 - y)][1:]
    for partner in partners:
        pl.semaphore_signal(barrier, inc=1, device_id={"ctx": partner}, device_id_type=pl.DeviceIdType.MESH)

    pl.semaphore_wait(barrier, len(partners))

    def first(ch, i):
        src = (k_in, v_in)[ch // CUT].at[pl.ds(ch % CUT * piece, piece)]
        return send(src, kv.at[rows(mine, ch)], first_sent.at[2 * ch + i], kvsem.at[mine * pieces + ch], (up, down)[i])

    for ch in range(pieces):
        for i in range(2):
            first(ch, i).start()
    for slot in (2, 1, 3, 4, 5):
        @pl.when(guest[slot // 2])
        def _(slot=slot):
            q_copy(slot).start()
    for copy in own:
        copy.wait()
    for ch in range(pieces):
        kv_send(mine, ch, twin)

    @pl.loop(0, SLOTS)
    def _(slot):
        for h in range(H):
            mx[slot, h] = jnp.full((sh, D), NEG, jnp.float32)
            tot[slot, h] = jnp.zeros((sh, D), jnp.float32)
            acc[slot, h] = jnp.zeros((sh, D), jnp.float32)

    def group(n):
        d = (n + 1) // 2
        back = n % 2
        return (z + back * (NZ - d) + (1 - back) * d) % NZ

    def attend(slot, g, masked):
        k = kv[pl.ds(pl.multiple_of(g * grp, grp), grp), :]
        v = kv[pl.ds(pl.multiple_of(vbase * sh + g * grp, grp), grp), :]
        if masked:
            q0 = home(slot) * sh
            k0 = ctx_of(x, g, y, 0) * sh
            qpos = q0 + lax.broadcasted_iota(jnp.int32, (sh, D), 0)
            lo = jnp.zeros((sh, D), jnp.int32)
            for i in range(3):
                lo = jnp.where(qpos >= docs[i], docs[i], lo)
            lane = lax.broadcasted_iota(jnp.int32, (sh, D), 1)
        def scores(h, b):
            q = qbuf[slot, b * ROWS:(b + 1) * ROWS, h * D:(h + 1) * D]
            return lax.dot_general(q, k, (((1,), (1,)), ((), ())), preferred_element_type=jnp.float32)

        def mask(s, b):
            parts = [s[:, j * D:(j + 1) * D] for j in range(grp // D)]
            if masked:
                here = slice(b * ROWS, (b + 1) * ROWS)
                parts = [
                    jnp.where(
                        (lane[here] + (k0 + j * D) <= qpos[here]) & (lane[here] + (k0 + j * D) >= lo[here]), part, NEG
                    )
                    for j, part in enumerate(parts)
                ]
            return parts

        def soft(s, h, b):
            here = slice(b * ROWS, (b + 1) * ROWS)
            parts = mask(s, b)
            top = functools.reduce(jnp.maximum, parts)
            old = mx[slot, h, here]
            new = jnp.maximum(old, jnp.max(top, axis=1, keepdims=True))
            mx[slot, h, here] = new
            new2 = new * C2
            parts = [jnp.exp2(part * C2 - new2) for part in parts]
            p = jnp.concatenate([part.astype(jnp.bfloat16) for part in parts], axis=1)
            decay = jnp.exp2(old * C2 - new2)
            tot[slot, h, here] = tot[slot, h, here] * decay + functools.reduce(jnp.add, parts)
            return p, decay

        def gather(p, decay, h, b):
            here = slice(b * ROWS, (b + 1) * ROWS)
            pv = jnp.dot(p, v, preferred_element_type=jnp.float32)
            acc[slot, h, here] = acc[slot, h, here] * decay + pv

        todo = [(h, b) for h in range(H) for b in range(sh // ROWS)]
        s = scores(*todo[0])
        for at, (h, b) in enumerate(todo):
            ahead = scores(*todo[at + 1]) if at + 1 < len(todo) else None
            p, decay = soft(s, h, b)
            gather(p, decay, h, b)
            s = ahead

    def task(slot, g):
        sx = slot // 2
        if_own = (sx == 0) & (g <= z) & jnp.logical_not((x == 1) & (z >= half) & (g < half))
        if_one = (sx == 1) & ((x == 2) | ((x == 1) & (g >= half)) | ((x == 0) & low))
        if_two = (sx == 2) & (x == 1) & (g >= half)
        needed = if_own | if_one | if_two
        masked = ((sx == 0) & (g == z)) | (x == 0) | ((sx == 0) & (x == 1) & low)

        @pl.when(needed & masked)
        def _():
            attend(slot, g, True)

        @pl.when(needed & jnp.logical_not(masked))
        def _():
            attend(slot, g, False)

    eye = lax.broadcasted_iota(jnp.int32, (D, D), 0) == lax.broadcasted_iota(jnp.int32, (D, D), 1)

    def finish(slot):
        for h in range(H):
            weight = jnp.broadcast_to(jnp.sum(tot[slot, h], axis=1, keepdims=True), (sh, D))
            osend[slot - 1, :, h * D:(h + 1) * D] = (acc[slot, h] / weight).astype(jnp.bfloat16)
            lse = mx[slot, h] * C2 + jnp.log2(weight)
            for b in range(sh // D):
                block = jnp.where(eye, lse[b * D:(b + 1) * D], 0.0)
                ssend[slot - 1, pl.ds(h * (sh // D) + b, 1), :] = jnp.sum(block, axis=0, keepdims=True)

    def o_copies(slot):
        to = home(slot)
        i = slot - 1
        return (
            send(osend.at[i], orecv.at[i], osent.at[i], osem.at[i], to),
            send(ssend.at[i], srecv.at[i], rsent.at[i], rsem.at[i], to),
        )

    @pl.loop(1, half + 2)
    def _(s):
        up_j = shard((z + NZ - s) % NZ, c)
        down_j = shard((z + s) % NZ, c)

        @pl.loop(0, pieces)
        def _(ch):
            late = ch // CUT
            last_up = half - late
            last_down = half - 1 + late

            @pl.when(s <= last_up)
            def _():
                kv_wait(up_j, ch)

                @pl.when(s < last_up)
                def _():
                    kv_send(up_j, ch, up)

            @pl.when(s <= last_down)
            def _():
                kv_wait(down_j, ch)

                @pl.when(s < last_down)
                def _():
                    kv_send(down_j, ch, down)

            @pl.when(s <= last_up)
            def _():
                kv_send(up_j, ch, twin)

            @pl.when(s <= last_down)
            def _():
                kv_send(down_j, ch, twin)

            n = 2 * s - 3 + ch // CUT

            @pl.when((n >= 0) & (n < NZ))
            def _():
                @pl.when(ch % CUT == 0)
                def _():
                    for part in range(pieces):
                        kv_wait(shard(group(n), 1 - c), part)

                @pl.loop(0, SLOTS // CUT)
                def _(t):
                    last = (n == NZ - 1).astype(jnp.int32)
                    slot = SLOTS - 1 - last * (3 * (ch % CUT) + t) - (1 - last) * (ch % CUT + 2 * t)
                    begin = jnp.array(BEGIN[0], jnp.int32)
                    for at in range(1, SLOTS):
                        begin = jnp.where(slot == at, BEGIN[at], begin)

                    @pl.when(hosted(slot) & (n >= begin))
                    def _():
                        @pl.when((slot > 0) & (n == begin))
                        def _():
                            q_copy(slot).wait_recv()

                        start = n * (n > begin).astype(jnp.int32)

                        @pl.loop(start, n + 1)
                        def _(k):
                            task(slot, group(k))

                        @pl.when((n == NZ - 1) & (slot > 0))
                        def _():
                            finish(slot)
                            for copy in o_copies(slot):
                                copy.start()

    def fold(slot):
        for copy in o_copies(slot):
            copy.wait_recv()
        for h in range(H):
            for b in range(sh // D):
                here = slice(b * D, (b + 1) * D)
                row = srecv[slot - 1, pl.ds(h * (sh // D) + b, 1), :]
                lse = jnp.broadcast_to(jnp.sum(jnp.where(eye, row, 0.0), axis=1, keepdims=True), (D, D))
                m2 = mx[0, h, here]
                best = jnp.maximum(m2, lse)
                keep = jnp.exp2(m2 - best)
                w = jnp.exp2(lse - best)
                part = orecv[slot - 1, here, h * D:(h + 1) * D].astype(jnp.float32)
                acc[0, h, here] = acc[0, h, here] * keep + part * w
                tot[0, h, here] = tot[0, h, here] * keep + w
                mx[0, h, here] = best

    for h in range(H):
        mx[0, h] = mx[0, h] * C2
        tot[0, h] = jnp.broadcast_to(jnp.sum(tot[0, h], axis=1, keepdims=True), (sh, D))

    fold(1)

    @pl.loop(0, SLOTS - 2)
    def _(t):
        slot = 2 + (t + 2) % 4

        @pl.when(((slot < 4) & guest[1]) | ((slot >= 4) & guest[2]))
        def _():
            fold(slot)

    for h in range(H):
        out[:, h * D:(h + 1) * D] = (acc[0, h] / tot[0, h]).astype(out.dtype)

    for slot in range(1, SLOTS):
        @pl.when(guest[slot // 2])
        def _(slot=slot):
            q_copy(slot).wait_send()

    for slot in range(1, SLOTS):
        @pl.when(host[slot // 2])
        def _(slot=slot):
            for copy in o_copies(slot):
                copy.wait_send()
    for ch in range(pieces):
        for i in range(2):
            first(ch, i).wait_send()
    send(kv.at[pl.ds(0, SENDS * sh)], kv.at[pl.ds(0, SENDS * sh)], kvsent, kvsem.at[0], twin).wait_send()


def shards(queries, keys, values, doc_starts):
    sh = keys.shape[0]
    any_spec = pl.BlockSpec(memory_space=pl.ANY)
    dma = pltpu.SemaphoreType.DMA
    return pl.pallas_call(
        kernel,
        out_shape=jax.ShapeDtypeStruct((sh, H * D), jnp.bfloat16),
        in_specs=[pl.BlockSpec(memory_space=pltpu.SMEM), any_spec, any_spec, any_spec],
        out_specs=pl.BlockSpec(memory_space=pltpu.VMEM),
        scratch_shapes=[
            pltpu.VMEM((SLOTS, sh, H * D), jnp.bfloat16),
            pltpu.VMEM((2 * NZ * NC * sh, D), jnp.bfloat16),
            pltpu.VMEM((SLOTS, H, sh, D), jnp.float32),
            pltpu.VMEM((SLOTS, H, sh, D), jnp.float32),
            pltpu.VMEM((SLOTS, H, sh, D), jnp.float32),
            pltpu.VMEM((SLOTS - 1, sh, H * D), jnp.bfloat16),
            pltpu.VMEM((SLOTS - 1, H * sh // D, D), jnp.float32),
            pltpu.VMEM((SLOTS - 1, sh, H * D), jnp.bfloat16),
            pltpu.VMEM((SLOTS - 1, H * sh // D, D), jnp.float32),
            dma((2 * CUT * NZ * NC,)), dma((SLOTS,)), dma((SLOTS - 1,)), dma((SLOTS - 1,)),
            dma, dma((4 * CUT,)), dma((SLOTS,)), dma((SLOTS - 1,)), dma((SLOTS - 1,)),
        ],
        compiler_params=pltpu.CompilerParams(collective_id=0, has_side_effects=True),
        name="ring_attention",
    )(doc_starts, queries, keys, values)


def solution(mesh):
    in_specs = (P("ctx", "head"), P("ctx", "head"), P("ctx", "head"), P("head"))
    out_specs = P("ctx", "head")
    return jax.shard_map(shards, mesh=mesh, in_specs=in_specs, out_specs=out_specs, check_vma=False)
```

time: 435 us -> 42.4 us (0.10)
  the two profiles are of different devices: /device:TPU:230 before, /device:TPU:5 now
where the time goes in v2:
time: 42.4 us; the launch traced here: 41.8 us
  Pallas kernels  40.3 us (95%)
  local copies, waits for them, and re-layouts  1.57 us (4%)
    pallas_call x1, Pallas kernels, shards(): pl.pallas_call(kernel, out_shape=jax.ShapeDtypeStruct((sh, H * D), jnp.bf...  40.3 us
    unnamed x1, local copies, waits for them, and re-layouts  1.57 us

profile of v2, /device:TPU:5, one launch (start us, length us, event | category | flops | bytes accessed | tf_op | source)
XLA Modules:
  0.0 41.8 jit_solution(5370135203790302162)
XLA Ops:
  0.0 40.3 %ring_attention.1 = bf16[256,256]{1,0:T(8,128)(2,1)} custom-call(s32[3]{0:T(128)} %docs.1, bf16[256,256]{1,0:T(8,128)(2,1)} %q_in.1, bf16[256,128]{1,0:T(8,128)(2,1)} %k_in.1, bf16[256,128]{1,0:T(8,128)(2,1)} %v_in.1), custom_call_target="tpu_custom_call" | custom-call | tf_op jit(solution)/shard_map/ring_attention/pallas_call | solution.py:341
  40.3 1.6 %copy.6 = bf16[256,256]{1,0:T(8,128)(2,1)} copy(bf16[256,256]{1,0:T(8,128)(2,1)} %ring_attention.1) | data formatting | bytes 262144

commit v3 on v2

--- a/solution.py
+++ b/solution.py
@@ -14,8 +14,8 @@
 PLANE = NZ * NY * NC
 SLOTS = 6
 ROWS = 256
-BEGIN = (7, 5, 1, 2, 3, 4)
-CUT = 2
+BEGIN = (7, 7, 1, 2, 3, 4)
+CUT = 1
 NEG = -1e30
 C2 = math.log2(math.e) / 12.0
 SENDS = 26
@@ -261,7 +261,7 @@
                 @pl.loop(0, SLOTS // CUT)
                 def _(t):
                     last = (n == NZ - 1).astype(jnp.int32)
-                    slot = SLOTS - 1 - last * (3 * (ch % CUT) + t) - (1 - last) * (ch % CUT + 2 * t)
+                    slot = SLOTS - 1 - last * (SLOTS // CUT * (ch % CUT) + t) - (1 - last) * (ch % CUT + CUT * t)
                     begin = jnp.array(BEGIN[0], jnp.int32)
                     for at in range(1, SLOTS):
                         begin = jnp.where(slot == at, BEGIN[at], begin)
@@ -278,7 +278,9 @@
                         def _(k):
                             task(slot, group(k))
 
-                        @pl.when((n == NZ - 1) & (slot > 0))
+                        early = ((x == 1) & (z >= half) & (slot > 1)).astype(jnp.int32)
+
+                        @pl.when((n == NZ - 1 - early) & (slot > 0))
                         def _():
                             finish(slot)
                             for copy in o_copies(slot):

time: 42.4 us -> 41.2 us (0.972); the launches traced: 41.8 us -> 41.1 us
  Pallas kernels: 40.3 us -> 39.5 us
    pallas_call x1, Pallas kernels: 40.3 us -> 39.5 us  [shards(): pl.pallas_call(kernel, out_shape=jax.ShapeDtypeStruct((sh, H * D), jnp.bf...]
where the time goes in v3:
time: 41.2 us; the launch traced here: 41.1 us
  Pallas kernels  39.5 us (96%)
  local copies, waits for them, and re-layouts  1.57 us (4%)
    pallas_call x1, Pallas kernels, shards(): pl.pallas_call(kernel, out_shape=jax.ShapeDtypeStruct((sh, H * D), jnp.bf...  39.5 us
    unnamed x1, local copies, waits for them, and re-layouts  1.57 us

profile of v3, /device:TPU:5, one launch (start us, length us, event | category | flops | bytes accessed | tf_op | source)
XLA Modules:
  0.0 41.1 jit_solution(17030928293097469404)
XLA Ops:
  0.0 39.5 %ring_attention.1 = bf16[256,256]{1,0:T(8,128)(2,1)} custom-call(s32[3]{0:T(128)} %docs.1, bf16[256,256]{1,0:T(8,128)(2,1)} %q_in.1, bf16[256,128]{1,0:T(8,128)(2,1)} %k_in.1, bf16[256,128]{1,0:T(8,128)(2,1)} %v_in.1), custom_call_target="tpu_custom_call" | custom-call | tf_op jit(solution)/shard_map/ring_attention/pallas_call | solution.py:343
  39.5 1.6 %copy.6 = bf16[256,256]{1,0:T(8,128)(2,1)} copy(bf16[256,256]{1,0:T(8,128)(2,1)} %ring_attention.1) | data formatting | bytes 262144

commit v4 on v3

--- a/solution.py
+++ b/solution.py
@@ -90,12 +90,23 @@
         return send(q_in, qbuf.at[slot], qsent.at[slot], qsem.at[slot], to)
 
     barrier = pltpu.get_barrier_semaphore()
-    partners = [up, down, twin]
-    partners += [ctx_of((x + dx) % NX, z, side, c) for dx in range(NX) for side in (y, 1 - y)][1:]
-    for partner in partners:
+    def greet(partner):
         pl.semaphore_signal(barrier, inc=1, device_id={"ctx": partner}, device_id_type=pl.DeviceIdType.MESH)
 
-    pl.semaphore_wait(barrier, len(partners))
+    for partner in (up, down, twin, ctx_of(x, z, 1 - y, c)):
+        greet(partner)
+    greeted = jnp.array(4, jnp.int32)
+    for dx in range(1, NX):
+        other = (x + dx) % NX
+        meets = ((x > 0) & (other > 0)) | (low & (x + other == 1))
+        greeted += 2 * meets.astype(jnp.int32)
+
+        @pl.when(meets)
+        def _(other=other):
+            for side in (y, 1 - y):
+                greet(ctx_of(other, z, side, c))
+
+    pl.semaphore_wait(barrier, greeted)
 
     def first(ch, i):
         src = (k_in, v_in)[ch // CUT].at[pl.ds(ch % CUT * piece, piece)]
@@ -108,10 +119,11 @@
         @pl.when(guest[slot // 2])
         def _(slot=slot):
             q_copy(slot).start()
+    for ch in range(pieces):
+        src = (k_in, v_in)[ch // CUT].at[pl.ds(ch % CUT * piece, piece)]
+        send(src, kv.at[rows(mine, ch)], kvsent, kvsem.at[mine * pieces + ch], twin).start()
     for copy in own:
         copy.wait()
-    for ch in range(pieces):
-        kv_send(mine, ch, twin)
 
     @pl.loop(0, SLOTS)
     def _(slot):
@@ -265,6 +277,7 @@
                     begin = jnp.array(BEGIN[0], jnp.int32)
                     for at in range(1, SLOTS):
                         begin = jnp.where(slot == at, BEGIN[at], begin)
+                    begin = jnp.where((x == NX - 1) & (slot == 1), 3, begin)
 
                     @pl.when(hosted(slot) & (n >= begin))
                     def _():
@@ -307,8 +320,6 @@
         mx[0, h] = mx[0, h] * C2
         tot[0, h] = jnp.broadcast_to(jnp.sum(tot[0, h], axis=1, keepdims=True), (sh, D))
 
-    fold(1)
-
     @pl.loop(0, SLOTS - 2)
     def _(t):
         slot = 2 + (t + 2) % 4
@@ -317,6 +328,7 @@
         def _():
             fold(slot)
 
+    fold(1)
     for h in range(H):
         out[:, h * D:(h + 1) * D] = (acc[0, h] / tot[0, h]).astype(out.dtype)
 

time: 41.2 us -> 41.3 us (level)
  no operation moved by 1% of the time
where the time goes in v4:
time: 41.3 us; the launch traced here: 41.2 us
  Pallas kernels  39.6 us (96%)
  local copies, waits for them, and re-layouts  1.57 us (4%)
    pallas_call x1, Pallas kernels, shards(): pl.pallas_call(kernel, out_shape=jax.ShapeDtypeStruct((sh, H * D), jnp.bf...  39.6 us
    unnamed x1, local copies, waits for them, and re-layouts  1.57 us

profile of v4, /device:TPU:5, one launch (start us, length us, event | category | flops | bytes accessed | tf_op | source)
XLA Modules:
  0.0 41.2 jit_solution(14287874504637374829)
XLA Ops:
  0.0 39.6 %ring_attention.1 = bf16[256,256]{1,0:T(8,128)(2,1)} custom-call(s32[3]{0:T(128)} %docs.1, bf16[256,256]{1,0:T(8,128)(2,1)} %q_in.1, bf16[256,128]{1,0:T(8,128)(2,1)} %k_in.1, bf16[256,128]{1,0:T(8,128)(2,1)} %v_in.1), custom_call_target="tpu_custom_call" | custom-call | tf_op jit(solution)/shard_map/ring_attention/pallas_call | solution.py:355
  39.6 1.6 %copy.6 = bf16[256,256]{1,0:T(8,128)(2,1)} copy(bf16[256,256]{1,0:T(8,128)(2,1)} %ring_attention.1) | data formatting | bytes 262144
